TPU v7x, 32 devices: a whole 2x2x4 slice. The times are simulated.
32 devices in a mesh: tau: 2 (over y), aux: 16 (over z, x, core).
Axes of the slice: x: 2, y: 2, z: 4, core: 2. Of those that a mesh axis runs over, the one named last changes fastest.
Arguments:
- coefficients: bfloat16 [16384, 2048], P('aux'), may hold values from -0.125 to 0.125
- green_occ: bfloat16 [16, 2048, 2048], P('tau', 'aux'), may hold values from -6 to 6
- green_vir: bfloat16 [16, 2048, 2048], P('tau', 'aux'), may hold values from -6 to 6
- minimax: float32 [16, 16], replicated, may hold values from -1.5 to 1.5
- coulomb: float32 [512], replicated, may hold values from 0.006 to 0.04
Outputs:
- screened: float32 [16, 16384, 512], P('tau', 'aux')
All inputs are finite; a program needn't handle non-finite values.
Results may differ from a plain program's by a relative error of at most 0.0078.
Values may be sent and summed in bfloat16 or wider, within the bound.
No kernel may reach another device: no remote copies, remote signals or barrier semaphores. Data moves between devices by JAX's collectives and lax.ppermute only.
A program may use at most 128 MiB of HBM per device.

v0:
```python
import jax
import jax.numpy as jnp
from jax import lax
from jax.sharding import PartitionSpec as P

NAUX = 16384
PANEL = 512
DYSON = 4


def per_device(coefficients, green_occ, green_vir, minimax, coulomb):
    stride = NAUX // PANEL
    local_panel = coefficients[::stride]
    panel_coef = lax.all_gather(local_panel, "aux", axis=0, tiled=True)
    product = (green_occ.astype(jnp.float32) * green_vir.astype(jnp.float32)).astype(jnp.bfloat16)
    folded = jnp.einsum(
        "tkn,qn->tkq", product, panel_coef, preferred_element_type=jnp.float32
    ).astype(jnp.bfloat16)
    owners = lax.axis_size("tau")
    freq_count = minimax.shape[0] // owners
    own_rows = lax.dynamic_slice_in_dim(minimax, lax.axis_index("tau") * freq_count, freq_count, 0)
    gathered = lax.all_gather(folded, "tau", axis=0, tiled=True)
    mixed = jnp.einsum(
        "wt,tkq->wkq", own_rows, gathered.astype(jnp.float32), precision=lax.Precision.HIGHEST
    )
    wide_coef = coefficients.astype(jnp.float32)
    chi_freq = jnp.einsum(
        "pk,wkq->wpq",
        wide_coef,
        lax.all_gather(mixed, "aux", axis=1, tiled=True),
        precision=lax.Precision.HIGHEST,
    )
    coupling = lax.all_gather(chi_freq[:, ::stride, :], "aux", axis=1, tiled=True)
    screened = chi_freq
    for sweep in range(DYSON):
        screened = chi_freq + jnp.einsum(
            "wpq,wqr->wpr", screened * coulomb, coupling, precision=lax.Precision.HIGHEST
        )
    return screened


def solution(mesh):
    placed = (P("aux", None), P("tau", "aux", None), P("tau", "aux", None), P(), P())
    return jax.shard_map(
        per_device, mesh=mesh, in_specs=placed, out_specs=P("tau", "aux", None), check_vma=False
    )
```

profile of v0, /device:TPU:0, one launch (start us, length us, event | category | flops | bytes accessed | tf_op | source)
XLA Modules:
  0.0 695.1 jit_solution(247652757352555016)
XLA Ops:
  6.5 3.0 slice.6
  9.5 0.0 all-gather.5.cloned.1.call-update
  9.5 0.0 all-gather.7.cloned.1.call-start
  9.6 44.3 %all-gather.5.cloned.1.call-done = bf16[512,2048]{1,0:T(8,128)(2,1)} async-done(((bf16[32,2048]{1,0:T(8,128)(2,1)}), bf16[512,2048]{1,0:T(8,128)(2,1)}) %all-gather.5.cloned.1.call-update) | async-done | bytes 2097168 | tf_op jit(solution)/shard_map/all_gather | solution.py:14
  53.9 7.4 %fusion.27 = bf16[8,128,512]{2,1,0:T(8,128)(2,1)} fusion(bf16[512,2048]{1,0:T(8,128)(2,1)} %all-gather.5.cloned.1.call-done, bf16[8,128,2048]{2,1,0:T(8,128)(2,1)} %param.7, bf16[8,128,2048]{2,1,0:T(8,128)(2,1)} %param.6), kind=kOutput, calls=%fused_computation.27 | convolution fusion | flops 2156396544 | bytes 11534336 | tf_op jit(solution)/shard_map/tkn,qn->tkq/dot_general | solution.py:16
  61.3 0.0 all-gather.7.cloned.1.call-update
  61.3 0.0 all-gather.9.cloned.1.call-start
  61.3 31.9 %all-gather.7.cloned.1.call-done = bf16[16,128,512]{2,1,0:T(8,128)(2,1)} async-done(((bf16[8,128,512]{2,1,0:T(8,128)(2,1)}), bf16[16,128,512]{2,1,0:T(8,128)(2,1)}) %all-gather.7.cloned.1.call-update) | async-done | bytes 2097168 | tf_op jit(solution)/shard_map/all_gather | solution.py:22
  93.3 3.5 fusion.25
  96.7 1.9 copy.16
  98.6 0.0 all-gather.9.cloned.1.call-update
  98.6 0.0 copy-start.3
  98.7 0.3 all-gather.11.cloned.1.call-start
  98.9 175.6 %all-gather.9.cloned.1.call-done = f32[8,2048,512]{1,2,0:T(8,128)} async-done(((f32[8,128,512]{1,2,0:T(8,128)}), f32[8,2048,512]{1,2,0:T(8,128)}) %all-gather.9.cloned.1.call-update) | async-done | bytes 33554448 | tf_op jit(solution)/shard_map/all_gather | solution.py:30
  274.5 59.4 %convolution_bitcast_fusion = f32[8,1024,512]{1,2,0:T(8,128)} fusion(f32[8,2048,512]{1,2,0:T(8,128)} %all-gather.9.cloned.1.call-done, bf16[1024,2048]{1,0:T(8,128)(2,1)} %param.5), kind=kOutput, calls=%fused_computation.12 | convolution fusion | flops 103079215104 | bytes 54525952 | tf_op jit(solution)/shard_map/pk,wkq->wpq/dot_general | solution.py:27
  333.9 27.1 %slice.7 = f32[8,32,512]{1,2,0:T(8,128)S(1)} slice(f32[8,1024,512]{1,2,0:T(8,128)} %convolution_bitcast_fusion), slice={[0:8:1], [0:1024:32], [0:512:1]} | slice | bytes 1048576 | tf_op jit(solution)/shard_map/slice | solution.py:33
  361.1 1.4 copy.10
  362.5 0.0 all-gather.11.cloned.1.call-update
  362.5 72.2 %all-gather.11.cloned.1.call-done = f32[8,512,512]{2,0,1:T(8,128)} async-done(((f32[8,32,512]{2,0,1:T(8,128)}), f32[8,512,512]{2,0,1:T(8,128)}) %all-gather.11.cloned.1.call-update) | async-done | bytes 8388624 | tf_op jit(solution)/shard_map/all_gather | solution.py:33
  434.8 75.6 %fusion.9 = f32[8,1024,512]{1,2,0:T(8,128)} fusion(f32[8,1024,512]{1,2,0:T(8,128)} %convolution_bitcast_fusion, f32[512]{0:T(512)S(1)} %copy-done.3, f32[8,512,512]{2,0,1:T(8,128)} %all-gather.11.cloned.1.call-done), kind=kOutput, calls=%fused_computation.9 | convolution fusion | flops 25773998080 | bytes 41945088 | tf_op jit(solution)/shard_map/wpq,wqr->wpr/dot_general | solution.py:36
  510.4 41.5 %fusion.6 = f32[8,1024,512]{1,2,0:T(8,128)} fusion(f32[8,1024,512]{1,2,0:T(8,128)} %convolution_bitcast_fusion, f32[8,1024,512]{1,2,0:T(8,128)} %fusion.9, f32[512]{0:T(512)S(1)} %copy-done.3, f32[8,512,512]{2,0,1:T(8,128)S(1)} %copy-done.2), kind=kOutput, calls=%fused_computation.6 | convolution fusion | flops 25778192384 | bytes 58722304 | tf_op jit(solution)/shard_map/wpq,wqr->wpr/dot_general | solution.py:36
  551.9 41.5 %fusion.3 = f32[8,1024,512]{1,2,0:T(8,128)} fusion(f32[8,1024,512]{1,2,0:T(8,128)} %convolution_bitcast_fusion, f32[8,1024,512]{1,2,0:T(8,128)} %fusion.6, f32[512]{0:T(512)S(1)} %copy-done.3, f32[8,512,512]{2,0,1:T(8,128)S(1)} %copy-done.2), kind=kOutput, calls=%fused_computation.3 | convolution fusion | flops 25778192384 | bytes 58722304 | tf_op jit(solution)/shard_map/wpq,wqr->wpr/dot_general | solution.py:36
  593.3 78.4 %fusion.11 = f32[8,1024,512]{1,2,0:T(8,128)} fusion(f32[8,1024,512]{1,2,0:T(8,128)} %convolution_bitcast_fusion, f32[8,1024,512]{1,2,0:T(8,128)} %fusion.3, f32[512]{0:T(512)S(1)} %copy-done.3, f32[8,512,512]{2,0,1:T(8,128)} %all-gather.11.cloned.1.call-done), kind=kOutput, calls=%fused_computation.11 | convolution fusion | flops 25782386688 | bytes 58722304 | tf_op jit(solution)/shard_map/wpq,wqr->wpr/dot_general | solution.py:36
  671.7 16.4 %copy.14 = f32[8,1024,512]{2,1,0:T(8,128)} copy(f32[8,1024,512]{1,2,0:T(8,128)} %fusion.11) | data formatting | bytes 33554432 | tf_op jit(solution)/shard_map/add | solution.py:36
  (8 shorter events, 0.0 us)
Async XLA Ops:
  6.5 86.7 %copy-start = (f32[16,16]{1,0:T(8,128)S(1)}, f32[16,16]{1,0:T(8,128)}, u32[]{:S(2)}) copy-start(f32[16,16]{1,0:T(8,128)} %param.8) | copy-start | bytes 3076
  6.5 47.3 %all-gather.5.cloned.1.call-start = ((), (), s32[]{:S(2)}) async-start(), calls=%async_computation | async-start | bytes 2228224 | tf_op jit(solution)/shard_map/all_gather | solution.py:14
  9.5 83.7 %all-gather.7.cloned.1.call-start = ((), (), s32[]{:S(2)}) async-start(), calls=%async_computation.1 | async-start | bytes 3145728 | tf_op jit(solution)/shard_map/all_gather | solution.py:22
  61.3 213.2 %all-gather.9.cloned.1.call-start = ((), (), s32[]{:S(2)}) async-start(), calls=%async_computation.2 | async-start | bytes 35651584 | tf_op jit(solution)/shard_map/all_gather | solution.py:30
  98.6 336.1 %copy-start.3 = (f32[512]{0:T(512)S(1)}, f32[512]{0:T(512)}, u32[]{:S(2)}) copy-start(f32[512]{0:T(512)} %param.9) | copy-start | bytes 6148
  98.7 336.1 %all-gather.11.cloned.1.call-start = ((), (), s32[]{:S(2)}) async-start(), calls=%async_computation.3 | async-start | bytes 8912896 | tf_op jit(solution)/shard_map/all_gather | solution.py:33
  434.8 75.6 %copy-start.2 = (f32[8,512,512]{2,0,1:T(8,128)S(1)}, f32[8,512,512]{2,0,1:T(8,128)}, u32[]{:S(2)}) copy-start(f32[8,512,512]{2,0,1:T(8,128)} %all-gather.11.cloned.1.call-done) | copy-start | bytes 25165828
  671.7 16.4 %copy-start.1 = (f32[16,16]{1,0:T(8,128)S(1)}, f32[16,16]{1,0:T(8,128)}, u32[]{:S(2)}) copy-start(f32[16,16]{1,0:T(8,128)} %param.8) | copy-start | bytes 3076
Sparse Core Ops, SparseCore 0:
  9.7 44.1 all-gather.4
  61.4 31.8 all-gather.6
  98.8 175.7 all-gather.8
  362.7 72.0 all-gather.10
where the time goes:
time: 700 us; the launch traced here: 695 us
  waiting for transfers between devices  324 us (46%)
  matrix products  307 us (44%)
  local copies, waits for them, and re-layouts  49.8 us (7%)
  between operations  13.6 us (2%)
    dot_general x4, matrix products, per_device(): jnp.einsum('wpq,wqr->wpr', screened * coulomb, coupling, precision=lax.Pr...  237 us
    all_gather x1, waiting for transfers between devices, per_device(): lax.all_gather(mixed, 'aux', axis=1, tiled=True)  176 us
    all_gather x1, waiting for transfers between devices, per_device(): lax.all_gather(chi_freq[:, ::stride, :], 'aux', axis=1, tiled=True)  72.2 us
    dot_general x1, matrix products, per_device(): jnp.einsum('pk,wkq->wpq', wide_coef, lax.all_gather(mixed, 'aux', axis=1,...  59.4 us
    all_gather x1, waiting for transfers between devices, per_device(): panel_coef = lax.all_gather(local_panel, 'aux', axis=0, tiled=True)  44.3 us
    all_gather x1, waiting for transfers between devices, per_device(): gathered = lax.all_gather(folded, 'tau', axis=0, tiled=True)  31.9 us
    slice x2, local copies, waits for them, and re-layouts, per_device(): chi_freq[:, ::stride, :]  28.6 us
    add x1, local copies, waits for them, and re-layouts, per_device(): chi_freq + jnp.einsum('wpq,wqr->wpr', screened * coulomb, coupling, preci...  16.4 us
  transfers between devices with their start and end apart: 4, of which 4 were waited for; matrix products, arithmetic and copies ran while one was open for 0% of the time, Pallas kernels for 0%

commit v1 on v0

v1 whole, which is shorter than its diff:
```python
import functools

import jax
import jax.numpy as jnp
from jax import lax
from jax.experimental import pallas as pl
from jax.experimental.pallas import tpu as pltpu
from jax.sharding import PartitionSpec as P

BF16 = jnp.bfloat16
F32 = jnp.float32
ANY = pl.BlockSpec(memory_space=pl.ANY)
NT = (((1,), (1,)), ((), ()))


def dot(a, b):
    return jnp.dot(a, b, preferred_element_type=F32)


def ring_tables(size):
    chips = size // 2
    order = [2 * z for z in range(chips // 2)] + [2 * z + 1 for z in reversed(range(chips // 2))]
    ahead = [
        (2 * order[i] + core, 2 * order[(i + 1) % chips] + core)
        for i in range(chips)
        for core in range(2)
    ]
    behind = [(b, a) for a, b in ahead]
    cores = [(i, i ^ 1) for i in range(size)]
    return ahead, behind, cores


def piece_owners(size, forward):
    chips = size // 2
    me = lax.axis_index("aux")
    chip, core = me // 2, me % 2
    level, side = chip // 2, chip % 2
    place = jnp.where(side == 0, level, chips - 1 - level)
    steps = jnp.asarray(piece_steps(chips, forward), jnp.int32)
    source = (place - steps + chips) % chips
    half = chips // 2
    owner = jnp.where(source < half, 2 * source, 2 * (chips - 1 - source) + 1)
    return jnp.concatenate([2 * owner + core, 2 * owner + (1 - core)]).astype(jnp.int32)


def piece_steps(chips, forward):
    far = chips // 2 if forward else chips - 1 - chips // 2
    return [0] + list(range(1, far + 1)) + [-s for s in range(1, chips - far)]


def ring_gather(own, size, forward):
    ahead, behind, cores = ring_tables(size)
    chips = size // 2
    far = chips // 2 if forward else chips - 1 - chips // 2
    up, down = [], []
    a = b = own
    for step in range(1, chips):
        if step <= far:
            a = lax.ppermute(a, "aux", ahead)
            up.append(a)
        if step < chips - far:
            b = lax.ppermute(b, "aux", behind)
            down.append(b)
    mine = [own] + up + down
    return mine + [lax.ppermute(m, "aux", cores) for m in mine]


def fold_kernel(count, parts, owners, product, *refs):
    pieces, outs, panel_out = refs[:count], refs[count : count + parts], refs[count + parts]
    panel, sems = refs[count + parts + 1 :]
    depth = pieces[0].shape[0]

    @pl.when(pl.program_id(0) == 0)
    def _():
        copies = []
        for i in range(count):
            offset = pl.multiple_of(owners[i] * depth, depth)
            copies.append(
                pltpu.make_async_copy(pieces[i], panel.at[pl.ds(offset, depth)], sems.at[i])
            )
        for copy in copies:
            copy.start()
        for copy in copies:
            copy.wait()
        panel_out[...] = panel[...]

    times, rows, points = product.shape
    left = product[...].reshape(times * rows, points)
    width = outs[0].shape[-1]
    for part in range(parts):
        right = panel[pl.ds(part * width, width), :]
        value = lax.dot_general(left, right, NT, preferred_element_type=F32)
        outs[part][...] = value.astype(BF16).reshape(times, rows, width)


def fold(product, pieces, owners, parts):
    times, rows, points = product.shape
    count = len(pieces)
    depth = pieces[0].shape[0]
    panel = count * depth
    width = panel // parts
    group = 2 if times % 2 == 0 else 1
    outs = [jax.ShapeDtypeStruct((times, rows, width), BF16)] * parts
    outs.append(jax.ShapeDtypeStruct((panel, points), BF16))
    return pl.pallas_call(
        functools.partial(fold_kernel, count, parts),
        out_shape=outs,
        grid_spec=pltpu.PrefetchScalarGridSpec(
            num_scalar_prefetch=1,
            grid=(times // group,),
            in_specs=[pl.BlockSpec((group, rows, points), lambda i, o: (i, 0, 0))] + [ANY] * count,
            out_specs=[pl.BlockSpec((group, rows, width), lambda i, o: (i, 0, 0))] * parts
            + [pl.BlockSpec((panel, points), lambda i, o: (0, 0))],
            scratch_shapes=[
                pltpu.VMEM((panel, points), BF16),
                pltpu.SemaphoreType.DMA((count,)),
            ],
        ),
        compiler_params=pltpu.CompilerParams(dimension_semantics=("arbitrary",)),
        name="fold",
    )(owners, product, *pieces)


def mix_kernel(groups, parts, place, weights, *refs):
    folded, outs = refs[:groups], refs[groups:]
    times, rows, width = folded[0].shape
    count = times * groups
    each = outs[0].shape[0]
    base = place[0] * (each * parts)
    strip, lanes = 16, 128

    def body(i, carry):
        at = pl.ds(pl.multiple_of(i * strip, strip), strip)
        for lane in range(0, width, lanes):
            cut = slice(lane, lane + lanes)
            values = [folded[g][t, at, cut].astype(F32) for g in range(groups) for t in range(times)]
            for w in range(each * parts):
                total = None
                for g in range(groups):
                    first = ((place[0] + g) % groups) * times
                    for t in range(times):
                        term = weights[base + w, first + t] * values[g * times + t]
                        total = term if total is None else total + term
                outs[w // each][w % each, at, cut] = total.astype(BF16)
        return carry

    lax.fori_loop(0, rows // strip, body, 0)


def mix(folded, minimax, place, parts):
    times, rows, width = folded[0].shape
    groups = len(folded)
    each = minimax.shape[0] // groups // parts
    return pl.pallas_call(
        functools.partial(mix_kernel, groups, parts),
        out_shape=[jax.ShapeDtypeStruct((each, rows, width), BF16)] * parts,
        in_specs=[pl.BlockSpec(memory_space=pltpu.SMEM)] * 2
        + [pl.BlockSpec(memory_space=pltpu.VMEM)] * groups,
        out_specs=[pl.BlockSpec(memory_space=pltpu.VMEM)] * parts,
        name="mix",
    )(place, minimax, *folded)


def fetch(owners, pieces, slots, sems, index, slot):
    depth = pieces[0].shape[1]
    copies = []
    for i, piece in enumerate(pieces):
        offset = pl.multiple_of(owners[i] * depth, depth)
        copies.append(
            pltpu.make_async_copy(
                piece.at[index], slots.at[slot, pl.ds(offset, depth)], sems.at[slot, i]
            )
        )
    return copies


def gathered(owners, pieces, slots, sems):
    step, steps = pl.program_id(0), pl.num_programs(0)
    slot = lax.rem(step, 2)

    @pl.when(step == 0)
    def _():
        for copy in fetch(owners, pieces, slots, sems, 0, 0):
            copy.start()

    for copy in fetch(owners, pieces, slots, sems, step, slot):
        copy.wait()

    @pl.when(step + 1 < steps)
    def _():
        for copy in fetch(owners, pieces, slots, sems, step + 1, 1 - slot):
            copy.start()

    return slots[slot]


def chi_kernel(count, owners, coef, panel, kernel, *refs):
    pieces = refs[:count]
    chi, step, slots, sems = refs[count:]
    right = gathered(owners, pieces, slots, sems)
    chi[0] = dot(coef[...], right).astype(BF16)
    step[0] = (dot(panel[...], right) * kernel[...]).astype(BF16)


def chi_first(coef, panel, kernel, pieces, owners):
    each, depth, width = pieces[0].shape
    rows, points = coef.shape
    size = panel.shape[0]
    count = len(pieces)
    once = pl.Buffered(1)
    return pl.pallas_call(
        functools.partial(chi_kernel, count),
        out_shape=[
            jax.ShapeDtypeStruct((each, rows, width), BF16),
            jax.ShapeDtypeStruct((each, size, width), BF16),
        ],
        grid_spec=pltpu.PrefetchScalarGridSpec(
            num_scalar_prefetch=1,
            grid=(each,),
            in_specs=[
                pl.BlockSpec((rows, points), lambda i, o: (0, 0), pipeline_mode=once),
                pl.BlockSpec((size, points), lambda i, o: (0, 0), pipeline_mode=once),
                pl.BlockSpec((size, 1), lambda i, o: (0, 0), pipeline_mode=once),
            ]
            + [ANY] * count,
            out_specs=[
                pl.BlockSpec((1, rows, width), lambda i, o: (i, 0, 0)),
                pl.BlockSpec((1, size, width), lambda i, o: (i, 0, 0)),
            ],
            scratch_shapes=[
                pltpu.VMEM((2, points, width), BF16),
                pltpu.SemaphoreType.DMA((2, count)),
            ],
        ),
        compiler_params=pltpu.CompilerParams(dimension_semantics=("arbitrary",)),
        name="chi",
    )(owners, coef, panel, kernel, *pieces)


def dyson_kernel(count, aliased, owners, coef, panel, kernel, chi_a, step_a, *refs):
    pieces = refs[:count]
    out, slots, sems = refs[count + aliased :]
    right = gathered(owners, pieces, slots, sems)
    chi_b = dot(coef[...], right)
    step_b = (dot(panel[...], right) * kernel[...]).astype(BF16)
    one = jnp.concatenate([step_a[0], step_b], axis=1)
    two = dot(one, one)
    pair = one.astype(F32) + two
    series = (pair + dot(two.astype(BF16), pair.astype(BF16))).astype(BF16)
    width = chi_b.shape[1]
    left = jnp.concatenate([chi_a[0], chi_b.astype(BF16)], axis=1)
    more = dot(left, series)
    out[0, :, :width] = chi_a[0].astype(F32) + more[:, :width]
    out[0, :, width:] = chi_b + more[:, width:]


def dyson(coef, panel, kernel, chi_a, step_a, pieces, owners, total, first, before):
    each, depth, width = pieces[0].shape
    rows, points = coef.shape
    size = panel.shape[0]
    count = len(pieces)
    once = pl.Buffered(1)
    extra = [] if before is None else [before]
    return pl.pallas_call(
        functools.partial(dyson_kernel, count, len(extra)),
        out_shape=jax.ShapeDtypeStruct((total, rows, size), F32),
        grid_spec=pltpu.PrefetchScalarGridSpec(
            num_scalar_prefetch=1,
            grid=(each,),
            in_specs=[
                pl.BlockSpec((rows, points), lambda i, o: (0, 0), pipeline_mode=once),
                pl.BlockSpec((size, points), lambda i, o: (0, 0), pipeline_mode=once),
                pl.BlockSpec((size, 1), lambda i, o: (0, 0), pipeline_mode=once),
                pl.BlockSpec((1, rows, width), lambda i, o: (i, 0, 0)),
                pl.BlockSpec((1, size, width), lambda i, o: (i, 0, 0)),
            ]
            + [ANY] * (count + len(extra)),
            out_specs=pl.BlockSpec((1, rows, size), lambda i, o: (first + i, 0, 0)),
            scratch_shapes=[
                pltpu.VMEM((2, points, width), BF16),
                pltpu.SemaphoreType.DMA((2, count)),
            ],
        ),
        input_output_aliases={} if before is None else {6 + count: 0},
        compiler_params=pltpu.CompilerParams(dimension_semantics=("arbitrary",)),
        name="dyson",
    )(owners, coef, panel, kernel, chi_a, step_a, *pieces, *extra)


def per_device(coefficients, green_occ, green_vir, minimax, coulomb):
    size, planes = lax.axis_size("aux"), lax.axis_size("tau")
    rows, points = coefficients.shape
    panel_size = coulomb.shape[0]
    stride = rows * size // panel_size
    place = lax.axis_index("tau")
    owners = {way: piece_owners(size, way) for way in (True, False)}
    kernel = coulomb[:, None]

    local = coefficients.reshape(rows // stride, stride, points)[:, 0, :]
    panel_pieces = ring_gather(local, size, True)
    product = (green_occ.astype(F32) * green_vir.astype(F32)).astype(BF16)
    parts = 2
    *folded, panel = fold(product, panel_pieces, owners[True], parts)

    freqs = minimax.shape[0] // planes
    splits = 2 if freqs % 2 == 0 else 1
    where = jnp.reshape(place, (1,)).astype(jnp.int32)
    chunks = []
    for part in range(parts):
        theirs = [
            lax.ppermute(folded[part], "tau", [((i + j) % planes, i) for i in range(planes)])
            for j in range(1, planes)
        ]
        chunks.append(mix([folded[part]] + theirs, minimax, where, splits))

    each = freqs // splits
    first = []
    for s in range(splits):
        way = s % 2 == 0
        pieces = ring_gather(chunks[0][s], size, way)
        first.append(chi_first(coefficients, panel, kernel, pieces, owners[way]))
    out = None
    for s in range(splits):
        way = s % 2 == 0
        pieces = ring_gather(chunks[1][s], size, way)
        chi_a, step_a = first[s]
        out = dyson(
            coefficients, panel, kernel, chi_a, step_a, pieces, owners[way], freqs, s * each, out
        )
    return out


def solution(mesh):
    placed = (P("aux", None), P("tau", "aux", None), P("tau", "aux", None), P(), P())
    return jax.shard_map(
        per_device, mesh=mesh, in_specs=placed, out_specs=P("tau", "aux", None), check_vma=False
    )
```

time: 700 us -> 222 us (0.32)
  matrix products: 307 us -> 0 us
  waiting for transfers between devices: 324 us -> 76.4 us
  Pallas kernels: 0 us -> 84.4 us
  starting transfers between devices: 0.35 us -> 46.1 us
  local copies, waits for them, and re-layouts: 49.8 us -> 4.5 us
  between operations: 13.6 us -> 0.96 us
  other arithmetic: 0 us -> 9.09 us
    all_gather x4 -> x0, waiting for transfers between devices: 324 us -> none  [the longest x1 176 us: per_device(): lax.all_gather(mixed, 'aux', axis=1, tiled=True)]
    dot_general x7 -> x0, matrix products: 307 us -> none  [the longest x4 237 us: per_device(): jnp.einsum('wpq,wqr->wpr', screened * coulomb, coupling, precision=lax.Pr...]
    pallas_call x0 -> x7, Pallas kernels: none -> 84.4 us  [the longest x2 37.5 us: dyson(): pl.pallas_call(functools.partial(dyson_kernel, count, len(extra)), out_sh...]
    ppermute x0 -> x77, waiting for transfers between devices: none -> 76.4 us  [the longest x18 39.9 us: ring_gather(): a = lax.ppermute(a, 'aux', ahead)]
    ppermute x0 -> x77, starting transfers between devices: none -> 46.1 us  [the longest x17 21.8 us: ring_gather(): b = lax.ppermute(b, 'aux', behind)]
    slice x3 -> x1, local copies, waits for them, and re-layouts: 31.5 us -> 1.38 us  [per_device(): local = coefficients.reshape(rows // stride, stride, points)[:, 0, :]]
    add x1 -> x0, local copies, waits for them, and re-layouts: 16.4 us -> none  [per_device(): chi_freq + jnp.einsum('wpq,wqr->wpr', screened * coulomb, coupling, preci...]
    convert_element_type x0 -> x1, other arithmetic: none -> 7.77 us  [per_device(): product = (green_occ.astype(F32) * green_vir.astype(F32)).astype(BF16)]
  transfers between devices with their start and end apart: 4 -> 77, of which waited for: 4 -> 33; matrix products, arithmetic and copies ran while one was open for 0% -> 5% of each run, Pallas kernels for 0% -> 26%
where the time goes in v1:
time: 222 us; the launch traced here: 221 us
  Pallas kernels  84.4 us (38%)
  waiting for transfers between devices  76.4 us (34%)
  starting transfers between devices  46.1 us (21%)
  other arithmetic  9.09 us (4%)
  local copies, waits for them, and re-layouts  4.5 us (2%)
    ppermute x18, waiting for transfers between devices, ring_gather(): a = lax.ppermute(a, 'aux', ahead)  39.9 us
    pallas_call x2, Pallas kernels, dyson(): pl.pallas_call(functools.partial(dyson_kernel, count, len(extra)), out_sh...  37.5 us
    pallas_call x2, Pallas kernels, chi_first(): pl.pallas_call(functools.partial(chi_kernel, count), out_shape=[jax.Shape...  27.1 us
    ppermute x17, starting transfers between devices, ring_gather(): b = lax.ppermute(b, 'aux', behind)  21.8 us
    ppermute x17, waiting for transfers between devices, ring_gather(): b = lax.ppermute(b, 'aux', behind)  21.4 us
    ppermute x18, starting transfers between devices, ring_gather(): a = lax.ppermute(a, 'aux', ahead)  18 us
    ppermute x2, waiting for transfers between devices, per_device(): lax.ppermute(folded[part], 'tau', [((i + j) % planes, i) for i in range(p...  14.7 us
    pallas_call x2, Pallas kernels, mix(): pl.pallas_call(functools.partial(mix_kernel, groups, parts), out_shape=[j...  11.8 us
  transfers between devices with their start and end apart: 77, of which 33 were waited for; matrix products, arithmetic and copies ran while one was open for 5% of the time, Pallas kernels for 26%

profile of v1, /device:TPU:0, one launch (start us, length us, event | category | flops | bytes accessed | tf_op | source)
XLA Modules:
  0.0 221.4 jit_solution(16408226222912526500)
XLA Ops:
  1.5 3.1 %collective-permute-start = (bf16[32,2048]{1,0:T(8,128)(2,1)S(1)}, bf16[32,2048]{1,0:T(8,128)(2,1)S(1)}, u32[]{:S(2)}, u32[]{:S(2)}) collective-permute-start(bf16[32,2048]{1,0:T(8,128)(2,1)S(1)} %bitcast.7), channel_id=1, source_target_pairs={{0,4},{1,5},{4,8},{5,9},{8,12},{9,13},{12,14},{13,15},{14,10},{15,... | collective-permute-start | bytes 393224 | tf_op jit(solution)/shard_map/ppermute | solution.py:59
  4.6 3.4 %collective-permute-done.refs_1_ = bf16[32,2048]{1,0:T(8,128)(2,1)S(1)} collective-permute-done((bf16[32,2048]{1,0:T(8,128)(2,1)S(1)}, bf16[32,2048]{1,0:T(8,128)(2,1)S(1)}, u32[]{:S(2)}, u32[]{:S(2)}) %collective-permute-start) | collective-permute-done | bytes 131104 | tf_op jit(solution)/shard_map/ppermute | solution.py:59
  10.1 2.9 %collective-permute-done.1.refs_2_ = bf16[32,2048]{1,0:T(8,128)(2,1)S(1)} collective-permute-done((bf16[32,2048]{1,0:T(8,128)(2,1)S(1)}, bf16[32,2048]{1,0:T(8,128)(2,1)S(1)}, u32[]{:S(2)}, u32[]{:S(2)}) %collective-permute-start.1) | collective-permute-done | bytes 131104 | tf_op jit(solution)/shard_map/ppermute | solution.py:59
  14.8 7.8 %multiply_convert_fusion.product = bf16[8,128,2048]{2,1,0:T(8,128)(2,1)} fusion(bf16[8,128,2048]{2,1,0:T(8,128)(2,1)} %param.9, bf16[8,128,2048]{2,1,0:T(8,128)(2,1)} %param.8), kind=kLoop, calls=%fused_computation | loop fusion | flops 8388608 | bytes 12582912 | tf_op jit(solution)/shard_map/convert_element_type | solution.py:301
  25.9 2.7 %collective-permute-done.6.refs_7_ = bf16[32,2048]{1,0:T(8,128)(2,1)S(1)} collective-permute-done((bf16[32,2048]{1,0:T(8,128)(2,1)S(1)}, bf16[32,2048]{1,0:T(8,128)(2,1)S(1)}, u32[]{:S(2)}, u32[]{:S(2)}) %collective-permute-start.6) | collective-permute-done | bytes 131104 | tf_op jit(solution)/shard_map/ppermute | solution.py:62
  31.3 8.1 %fold.1 = (bf16[8,128,256]{2,1,0:T(8,128)(2,1)}, bf16[8,128,256]{2,1,0:T(8,128)(2,1)}, bf16[512,2048]{1,0:T(8,128)(2,1)}) custom-call(s32[16]{0:T(128)} %pad_add_fusion.1.owners, bf16[8,128,2048]{2,1,0:T(8,128)(2,1)} %multiply_convert_fusion.product, bf16[32,2048]{1,0:T(8,128)(2,1)} %bitcast.10, bf16[32,2048]{1,0:T(8,128)(2,1)} %copy-done.48, ...), custom_call_target="tpu_custom_call" | custom-call | tf_op jit(solution)/shard_map/fold/pallas_call | solution.py:105
  41.6 13.0 %collective-permute-done.15.refs_1_ = bf16[8,128,256]{2,1,0:T(8,128)(2,1)S(1)} collective-permute-done((bf16[8,128,256]{2,1,0:T(8,128)(2,1)}, bf16[8,128,256]{2,1,0:T(8,128)(2,1)S(1)}, u32[]{:S(2)}, u32[]{:S(2)}) %collective-permute-start.15) | collective-permute-done | bytes 524320 | tf_op jit(solution)/shard_map/ppermute | solution.py:311
  55.3 5.9 %mix.2 = (bf16[4,128,256]{2,1,0:T(8,128)(2,1)}, bf16[4,128,256]{2,1,0:T(8,128)(2,1)}) custom-call(s32[1]{0:T(128)} %bitcast.3.place, f32[16,16]{1,0:T(8,128)} %weights.3, bf16[8,128,256]{2,1,0:T(8,128)(2,1)} %get-tuple-element.17.refs_0_, bf16[8,128,256]{2,1,0:T(8,128)(2,1)} %copy-done.2), custom_call_target="tpu_custom_call" | custom-call | tf_op jit(solution)/shard_map/mix/pallas_call | solution.py:154
  66.4 5.9 %mix.3 = (bf16[4,128,256]{2,1,0:T(8,128)(2,1)}, bf16[4,128,256]{2,1,0:T(8,128)(2,1)}) custom-call(s32[1]{0:T(128)} %bitcast.3.place, f32[16,16]{1,0:T(8,128)} %weights.3, bf16[8,128,256]{2,1,0:T(8,128)(2,1)} %get-tuple-element.21.refs_0_, bf16[8,128,256]{2,1,0:T(8,128)(2,1)} %copy-done.1), custom_call_target="tpu_custom_call" | custom-call | tf_op jit(solution)/shard_map/mix/pallas_call | solution.py:154
  75.8 5.9 %collective-permute-done.47.refs_1_ = bf16[4,128,256]{2,1,0:T(8,128)(2,1)S(1)} collective-permute-done((bf16[4,128,256]{2,1,0:T(8,128)(2,1)}, bf16[4,128,256]{2,1,0:T(8,128)(2,1)S(1)}, u32[]{:S(2)}, u32[]{:S(2)}) %collective-permute-start.47) | collective-permute-done | bytes 262176 | tf_op jit(solution)/shard_map/ppermute | solution.py:59
  83.7 3.6 %collective-permute-done.32.refs_1_ = bf16[4,128,256]{2,1,0:T(8,128)(2,1)S(1)} collective-permute-done((bf16[4,128,256]{2,1,0:T(8,128)(2,1)}, bf16[4,128,256]{2,1,0:T(8,128)(2,1)S(1)}, u32[]{:S(2)}, u32[]{:S(2)}) %collective-permute-start.32) | collective-permute-done | bytes 262176 | tf_op jit(solution)/shard_map/ppermute | solution.py:59
  95.1 3.2 %collective-permute-done.17.refs_2_ = bf16[4,128,256]{2,1,0:T(8,128)(2,1)S(1)} collective-permute-done((bf16[4,128,256]{2,1,0:T(8,128)(2,1)S(1)}, bf16[4,128,256]{2,1,0:T(8,128)(2,1)S(1)}, u32[]{:S(2)}, u32[]{:S(2)}) %collective-permute-start.17) | collective-permute-done | bytes 262176 | tf_op jit(solution)/shard_map/ppermute | solution.py:59
  104.9 2.6 %collective-permute-done.36.refs_5_ = bf16[4,128,256]{2,1,0:T(8,128)(2,1)S(1)} collective-permute-done((bf16[4,128,256]{2,1,0:T(8,128)(2,1)S(1)}, bf16[4,128,256]{2,1,0:T(8,128)(2,1)S(1)}, u32[]{:S(2)}, u32[]{:S(2)}) %collective-permute-start.36) | collective-permute-done | bytes 262176 | tf_op jit(solution)/shard_map/ppermute | solution.py:62
  110.5 2.6 %collective-permute-done.67.refs_6_ = bf16[4,128,256]{2,1,0:T(8,128)(2,1)S(1)} collective-permute-done((bf16[4,128,256]{2,1,0:T(8,128)(2,1)S(1)}, bf16[4,128,256]{2,1,0:T(8,128)(2,1)S(1)}, u32[]{:S(2)}, u32[]{:S(2)}) %collective-permute-start.67) | collective-permute-done | bytes 262176 | tf_op jit(solution)/shard_map/ppermute | solution.py:62
  113.2 3.1 %collective-permute-done.63.refs_2_ = bf16[4,128,256]{2,1,0:T(8,128)(2,1)S(1)} collective-permute-done((bf16[4,128,256]{2,1,0:T(8,128)(2,1)S(1)}, bf16[4,128,256]{2,1,0:T(8,128)(2,1)S(1)}, u32[]{:S(2)}, u32[]{:S(2)}) %collective-permute-start.63) | collective-permute-done | bytes 262176 | tf_op jit(solution)/shard_map/ppermute | solution.py:59
  119.2 3.1 %collective-permute-done.18.refs_3_ = bf16[4,128,256]{2,1,0:T(8,128)(2,1)S(1)} collective-permute-done((bf16[4,128,256]{2,1,0:T(8,128)(2,1)S(1)}, bf16[4,128,256]{2,1,0:T(8,128)(2,1)S(1)}, u32[]{:S(2)}, u32[]{:S(2)}) %collective-permute-start.18) | collective-permute-done | bytes 262176 | tf_op jit(solution)/shard_map/ppermute | solution.py:59
  128.0 3.6 %collective-permute-done.37.refs_6_ = bf16[4,128,256]{2,1,0:T(8,128)(2,1)S(1)} collective-permute-done((bf16[4,128,256]{2,1,0:T(8,128)(2,1)S(1)}, bf16[4,128,256]{2,1,0:T(8,128)(2,1)S(1)}, u32[]{:S(2)}, u32[]{:S(2)}) %collective-permute-start.37) | collective-permute-done | bytes 262176 | tf_op jit(solution)/shard_map/ppermute | solution.py:62
  139.3 3.2 %collective-permute-done.22.refs_7_ = bf16[4,128,256]{2,1,0:T(8,128)(2,1)} collective-permute-done((bf16[4,128,256]{2,1,0:T(8,128)(2,1)S(1)}, bf16[4,128,256]{2,1,0:T(8,128)(2,1)}, u32[]{:S(2)}, u32[]{:S(2)}) %collective-permute-start.22) | collective-permute-done | bytes 262176 | tf_op jit(solution)/shard_map/ppermute | solution.py:62
  145.0 3.2 %collective-permute-done.50.refs_4_ = bf16[4,128,256]{2,1,0:T(8,128)(2,1)} collective-permute-done((bf16[4,128,256]{2,1,0:T(8,128)(2,1)S(1)}, bf16[4,128,256]{2,1,0:T(8,128)(2,1)}, u32[]{:S(2)}, u32[]{:S(2)}) %collective-permute-start.50) | collective-permute-done | bytes 262176 | tf_op jit(solution)/shard_map/ppermute | solution.py:59
  150.3 3.0 %collective-permute-done.65.refs_4_ = bf16[4,128,256]{2,1,0:T(8,128)(2,1)} collective-permute-done((bf16[4,128,256]{2,1,0:T(8,128)(2,1)}, bf16[4,128,256]{2,1,0:T(8,128)(2,1)}, u32[]{:S(2)}, u32[]{:S(2)}) %collective-permute-start.65) | collective-permute-done | bytes 262176 | tf_op jit(solution)/shard_map/ppermute | solution.py:59
  156.5 13.5 %chi.3 = (bf16[4,1024,256]{2,1,0:T(8,128)(2,1)}, bf16[4,512,256]{2,1,0:T(8,128)(2,1)}) custom-call(s32[16]{0:T(128)} %pad_add_fusion.1.owners, bf16[1024,2048]{1,0:T(8,128)(2,1)} %coef.7, bf16[512,2048]{1,0:T(8,128)(2,1)} %get-tuple-element.16.panel, f32[512,1]{1,0:T(8,128)} %copy.13.kernel, bf16[4,128,256]{2,1,0:T(8,128)(2,1)} %get-tuple-element.23.refs_0_, ...), custom_call_target="tpu_custom_call" | custom-call | tf_op jit(solution)/shard_map/chi/pallas_call | solution.py:211
  170.2 13.5 %chi.2 = (bf16[4,1024,256]{2,1,0:T(8,128)(2,1)}, bf16[4,512,256]{2,1,0:T(8,128)(2,1)}) custom-call(s32[16]{0:T(128)} %pad_add_fusion.owners, bf16[1024,2048]{1,0:T(8,128)(2,1)} %coef.7, bf16[512,2048]{1,0:T(8,128)(2,1)} %get-tuple-element.16.panel, f32[512,1]{1,0:T(8,128)} %copy.13.kernel, bf16[4,128,256]{2,1,0:T(8,128)(2,1)} %get-tuple-element.18.refs_0_, ...), custom_call_target="tpu_custom_call" | custom-call | tf_op jit(solution)/shard_map/chi/pallas_call | solution.py:211
  183.7 18.7 %dyson.2.refs_16_ = f32[8,1024,512]{2,1,0:T(8,128)} custom-call(s32[16]{0:T(128)} %pad_add_fusion.1.owners, bf16[1024,2048]{1,0:T(8,128)(2,1)} %coef.7, bf16[512,2048]{1,0:T(8,128)(2,1)} %get-tuple-element.16.panel, f32[512,1]{1,0:T(8,128)} %copy.13.kernel, bf16[4,1024,256]{2,1,0:T(8,128)(2,1)} %get-tuple-element.24.chi_a, ...), custom_call_target="tpu_custom_call" | custom-call | tf_op jit(solution)/shard_map/dyson/pallas_call | solution.py:264
  202.5 18.7 %dyson.3 = f32[8,1024,512]{2,1,0:T(8,128)} custom-call(s32[16]{0:T(128)} %pad_add_fusion.owners, bf16[1024,2048]{1,0:T(8,128)(2,1)} %coef.7, bf16[512,2048]{1,0:T(8,128)(2,1)} %get-tuple-element.16.panel, f32[512,1]{1,0:T(8,128)} %copy.13.kernel, bf16[4,1024,256]{2,1,0:T(8,128)(2,1)} %get-tuple-element.19.chi_a, ...), custom_call_target="tpu_custom_call", output_to_operand_aliasing={{}: (22, {})} | custom-call | tf_op jit(solution)/shard_map/dyson/pallas_call | solution.py:264
  (278 shorter events, 66.2 us)
Async XLA Ops:
  9.9 15.3 %collective-permute-start.7 = (bf16[32,2048]{1,0:T(8,128)(2,1)S(1)}, bf16[32,2048]{1,0:T(8,128)(2,1)S(1)}, u32[]{:S(2)}, u32[]{:S(2)}) collective-permute-start(bf16[32,2048]{1,0:T(8,128)(2,1)S(1)} %bitcast.9), channel_id=1, source_target_pairs={{0,1},{1,0},{2,3},{3,2},{4,5},{5,4},{6,7},{7,6},{8,9},{9,8},{10,11... | collective-permute-start | bytes 393224 | tf_op jit(solution)/shard_map/ppermute | solution.py:65
  9.9 13.2 %collective-permute-start.5 = (bf16[32,2048]{1,0:T(8,128)(2,1)S(1)}, bf16[32,2048]{1,0:T(8,128)(2,1)S(1)}, u32[]{:S(2)}, u32[]{:S(2)}) collective-permute-start(bf16[32,2048]{1,0:T(8,128)(2,1)S(1)} %collective-permute-done.4.refs_5_), channel_id=1, source_target_pairs={{4,0},{5,1},{8,4},{9,5},{12,8},{13,9},{14,12},{15,13},{10,14},{11,... | collective-permute-start | bytes 393224 | tf_op jit(solution)/shard_map/ppermute | solution.py:62
  13.0 10.3 %collective-permute-start.2 = (bf16[32,2048]{1,0:T(8,128)(2,1)S(1)}, bf16[32,2048]{1,0:T(8,128)(2,1)S(1)}, u32[]{:S(2)}, u32[]{:S(2)}) collective-permute-start(bf16[32,2048]{1,0:T(8,128)(2,1)S(1)} %collective-permute-done.1.refs_2_), channel_id=1, source_target_pairs={{0,4},{1,5},{4,8},{5,9},{8,12},{9,13},{12,14},{13,15},{14,10},{15,... | collective-permute-start | bytes 393224 | tf_op jit(solution)/shard_map/ppermute | solution.py:59
  39.5 15.1 %collective-permute-start.15 = (bf16[8,128,256]{2,1,0:T(8,128)(2,1)}, bf16[8,128,256]{2,1,0:T(8,128)(2,1)S(1)}, u32[]{:S(2)}, u32[]{:S(2)}) collective-permute-start(bf16[8,128,256]{2,1,0:T(8,128)(2,1)} %get-tuple-element.17.refs_0_), channel_id=1, source_target_pairs={{16,0},{0,16},{17,1},{1,17},{18,2},{2,18},{19,3},{3,19},{20,4},{4,... | collective-permute-start | bytes 1572872 | tf_op jit(solution)/shard_map/ppermute | solution.py:311
  41.1 23.9 %collective-permute-start.31 = (bf16[8,128,256]{2,1,0:T(8,128)(2,1)}, bf16[8,128,256]{2,1,0:T(8,128)(2,1)S(1)}, u32[]{:S(2)}, u32[]{:S(2)}) collective-permute-start(bf16[8,128,256]{2,1,0:T(8,128)(2,1)} %get-tuple-element.21.refs_0_), channel_id=1, source_target_pairs={{16,0},{0,16},{17,1},{1,17},{18,2},{2,18},{19,3},{3,19},{20,4},{4,... | collective-permute-start | bytes 1572872 | tf_op jit(solution)/shard_map/ppermute | solution.py:311
  61.2 11.1 %collective-permute-start.23 = (bf16[4,128,256]{2,1,0:T(8,128)(2,1)}, bf16[4,128,256]{2,1,0:T(8,128)(2,1)S(1)}, u32[]{:S(2)}, u32[]{:S(2)}) collective-permute-start(bf16[4,128,256]{2,1,0:T(8,128)(2,1)} %get-tuple-element.18.refs_0_), channel_id=1, source_target_pairs={{0,1},{1,0},{2,3},{3,2},{4,5},{5,4},{6,7},{7,6},{8,9},{9,8},{10,11... | collective-permute-start | bytes 786440 | tf_op jit(solution)/shard_map/ppermute | solution.py:65
  61.2 12.0 %collective-permute-start.19 = (bf16[4,128,256]{2,1,0:T(8,128)(2,1)}, bf16[4,128,256]{2,1,0:T(8,128)(2,1)S(1)}, u32[]{:S(2)}, u32[]{:S(2)}) collective-permute-start(bf16[4,128,256]{2,1,0:T(8,128)(2,1)} %get-tuple-element.18.refs_0_), channel_id=1, source_target_pairs={{4,0},{5,1},{8,4},{9,5},{12,8},{13,9},{14,12},{15,13},{10,14},{11,... | collective-permute-start | bytes 786440 | tf_op jit(solution)/shard_map/ppermute | solution.py:62
  62.3 11.0 %collective-permute-start.16 = (bf16[4,128,256]{2,1,0:T(8,128)(2,1)}, bf16[4,128,256]{2,1,0:T(8,128)(2,1)S(1)}, u32[]{:S(2)}, u32[]{:S(2)}) collective-permute-start(bf16[4,128,256]{2,1,0:T(8,128)(2,1)} %get-tuple-element.18.refs_0_), channel_id=1, source_target_pairs={{0,4},{1,5},{4,8},{5,9},{8,12},{9,13},{12,14},{13,15},{14,10},{15,... | collective-permute-start | bytes 786440 | tf_op jit(solution)/shard_map/ppermute | solution.py:59
  63.2 11.2 %collective-permute-start.54 = (bf16[4,128,256]{2,1,0:T(8,128)(2,1)}, bf16[4,128,256]{2,1,0:T(8,128)(2,1)S(1)}, u32[]{:S(2)}, u32[]{:S(2)}) collective-permute-start(bf16[4,128,256]{2,1,0:T(8,128)(2,1)} %get-tuple-element.23.refs_0_), channel_id=1, source_target_pairs={{0,1},{1,0},{2,3},{3,2},{4,5},{5,4},{6,7},{7,6},{8,9},{9,8},{10,11... | collective-permute-start | bytes 786440 | tf_op jit(solution)/shard_map/ppermute | solution.py:65
  65.0 10.8 %collective-permute-start.51 = (bf16[4,128,256]{2,1,0:T(8,128)(2,1)}, bf16[4,128,256]{2,1,0:T(8,128)(2,1)S(1)}, u32[]{:S(2)}, u32[]{:S(2)}) collective-permute-start(bf16[4,128,256]{2,1,0:T(8,128)(2,1)} %get-tuple-element.23.refs_0_), channel_id=1, source_target_pairs={{4,0},{5,1},{8,4},{9,5},{12,8},{13,9},{14,12},{15,13},{10,14},{11,... | collective-permute-start | bytes 786440 | tf_op jit(solution)/shard_map/ppermute | solution.py:62
  73.2 10.0 %collective-permute-start.39 = (bf16[4,128,256]{2,1,0:T(8,128)(2,1)}, bf16[4,128,256]{2,1,0:T(8,128)(2,1)S(1)}, u32[]{:S(2)}, u32[]{:S(2)}) collective-permute-start(bf16[4,128,256]{2,1,0:T(8,128)(2,1)} %get-tuple-element.22.refs_0_), channel_id=1, source_target_pairs={{0,1},{1,0},{2,3},{3,2},{4,5},{5,4},{6,7},{7,6},{8,9},{9,8},{10,11... | collective-permute-start | bytes 786440 | tf_op jit(solution)/shard_map/ppermute | solution.py:65
  73.3 10.4 %collective-permute-start.35 = (bf16[4,128,256]{2,1,0:T(8,128)(2,1)}, bf16[4,128,256]{2,1,0:T(8,128)(2,1)S(1)}, u32[]{:S(2)}, u32[]{:S(2)}) collective-permute-start(bf16[4,128,256]{2,1,0:T(8,128)(2,1)} %get-tuple-element.22.refs_0_), channel_id=1, source_target_pairs={{4,0},{5,1},{8,4},{9,5},{12,8},{13,9},{14,12},{15,13},{10,14},{11,... | collective-permute-start | bytes 786440 | tf_op jit(solution)/shard_map/ppermute | solution.py:62
  74.4 12.9 %collective-permute-start.32 = (bf16[4,128,256]{2,1,0:T(8,128)(2,1)}, bf16[4,128,256]{2,1,0:T(8,128)(2,1)S(1)}, u32[]{:S(2)}, u32[]{:S(2)}) collective-permute-start(bf16[4,128,256]{2,1,0:T(8,128)(2,1)} %get-tuple-element.22.refs_0_), channel_id=1, source_target_pairs={{0,4},{1,5},{4,8},{5,9},{8,12},{9,13},{12,14},{13,15},{14,10},{15,... | collective-permute-start | bytes 786440 | tf_op jit(solution)/shard_map/ppermute | solution.py:59
  75.8 13.1 %collective-permute-start.69 = (bf16[4,128,256]{2,1,0:T(8,128)(2,1)}, bf16[4,128,256]{2,1,0:T(8,128)(2,1)S(1)}, u32[]{:S(2)}, u32[]{:S(2)}) collective-permute-start(bf16[4,128,256]{2,1,0:T(8,128)(2,1)} %get-tuple-element.26.refs_0_), channel_id=1, source_target_pairs={{0,1},{1,0},{2,3},{3,2},{4,5},{5,4},{6,7},{7,6},{8,9},{9,8},{10,11... | collective-permute-start | bytes 786440 | tf_op jit(solution)/shard_map/ppermute | solution.py:65
  103.3 9.8 %collective-permute-start.67 = (bf16[4,128,256]{2,1,0:T(8,128)(2,1)S(1)}, bf16[4,128,256]{2,1,0:T(8,128)(2,1)S(1)}, u32[]{:S(2)}, u32[]{:S(2)}) collective-permute-start(bf16[4,128,256]{2,1,0:T(8,128)(2,1)S(1)} %collective-permute-done.66.refs_5_), channel_id=1, source_target_pairs={{4,0},{5,1},{8,4},{9,5},{12,8},{13,9},{14,12},{15,13},{10,14},{11,... | collective-permute-start | bytes 786440 | tf_op jit(solution)/shard_map/ppermute | solution.py:62
  118.3 9.7 %collective-permute-start.49 = (bf16[4,128,256]{2,1,0:T(8,128)(2,1)S(1)}, bf16[4,128,256]{2,1,0:T(8,128)(2,1)S(1)}, u32[]{:S(2)}, u32[]{:S(2)}) collective-permute-start(bf16[4,128,256]{2,1,0:T(8,128)(2,1)S(1)} %collective-permute-done.48.refs_2_), channel_id=1, source_target_pairs={{0,4},{1,5},{4,8},{5,9},{8,12},{9,13},{12,14},{13,15},{14,10},{15,... | collective-permute-start | bytes 786440 | tf_op jit(solution)/shard_map/ppermute | solution.py:59
  125.6 10.8 %collective-permute-start.68 = (bf16[4,128,256]{2,1,0:T(8,128)(2,1)S(1)}, bf16[4,128,256]{2,1,0:T(8,128)(2,1)}, u32[]{:S(2)}, u32[]{:S(2)}) collective-permute-start(bf16[4,128,256]{2,1,0:T(8,128)(2,1)S(1)} %collective-permute-done.67.refs_6_), channel_id=1, source_target_pairs={{4,0},{5,1},{8,4},{9,5},{12,8},{13,9},{14,12},{15,13},{10,14},{11,... | collective-permute-start | bytes 786440 | tf_op jit(solution)/shard_map/ppermute | solution.py:62
  144.5 9.9 %collective-permute-start.76 = (bf16[4,128,256]{2,1,0:T(8,128)(2,1)}, bf16[4,128,256]{2,1,0:T(8,128)(2,1)}, u32[]{:S(2)}, u32[]{:S(2)}) collective-permute-start(bf16[4,128,256]{2,1,0:T(8,128)(2,1)} %collective-permute-done.68.refs_7_), channel_id=1, source_target_pairs={{0,1},{1,0},{2,3},{3,2},{4,5},{5,4},{6,7},{7,6},{8,9},{9,8},{10,11... | collective-permute-start | bytes 786440 | tf_op jit(solution)/shard_map/ppermute | solution.py:65
  144.5 10.4 %collective-permute-start.72 = (bf16[4,128,256]{2,1,0:T(8,128)(2,1)}, bf16[4,128,256]{2,1,0:T(8,128)(2,1)}, u32[]{:S(2)}, u32[]{:S(2)}) collective-permute-start(bf16[4,128,256]{2,1,0:T(8,128)(2,1)} %collective-permute-done.64.refs_3_), channel_id=1, source_target_pairs={{0,1},{1,0},{2,3},{3,2},{4,5},{5,4},{6,7},{7,6},{8,9},{9,8},{10,11... | collective-permute-start | bytes 786440 | tf_op jit(solution)/shard_map/ppermute | solution.py:65
  154.4 48.1 %collective-permute-start.44 = (bf16[4,128,256]{2,1,0:T(8,128)(2,1)S(1)}, bf16[4,128,256]{2,1,0:T(8,128)(2,1)}, u32[]{:S(2)}, u32[]{:S(2)}) collective-permute-start(bf16[4,128,256]{2,1,0:T(8,128)(2,1)S(1)} %collective-permute-done.36.refs_5_), channel_id=1, source_target_pairs={{0,1},{1,0},{2,3},{3,2},{4,5},{5,4},{6,7},{7,6},{8,9},{9,8},{10,11... | collective-permute-start | bytes 786440 | tf_op jit(solution)/shard_map/ppermute | solution.py:65
  154.9 47.6 %collective-permute-start.41 = (bf16[4,128,256]{2,1,0:T(8,128)(2,1)S(1)}, bf16[4,128,256]{2,1,0:T(8,128)(2,1)}, u32[]{:S(2)}, u32[]{:S(2)}) collective-permute-start(bf16[4,128,256]{2,1,0:T(8,128)(2,1)S(1)} %collective-permute-done.33.refs_2_), channel_id=1, source_target_pairs={{0,1},{1,0},{2,3},{3,2},{4,5},{5,4},{6,7},{7,6},{8,9},{9,8},{10,11... | collective-permute-start | bytes 786440 | tf_op jit(solution)/shard_map/ppermute | solution.py:65
  154.9 47.6 %collective-permute-start.45 = (bf16[4,128,256]{2,1,0:T(8,128)(2,1)}, bf16[4,128,256]{2,1,0:T(8,128)(2,1)}, u32[]{:S(2)}, u32[]{:S(2)}) collective-permute-start(bf16[4,128,256]{2,1,0:T(8,128)(2,1)} %copy-done.17), channel_id=1, source_target_pairs={{0,1},{1,0},{2,3},{3,2},{4,5},{5,4},{6,7},{7,6},{8,9},{9,8},{10,11... | collective-permute-start | bytes 786440 | tf_op jit(solution)/shard_map/ppermute | solution.py:65
  155.4 47.1 %collective-permute-start.42 = (bf16[4,128,256]{2,1,0:T(8,128)(2,1)}, bf16[4,128,256]{2,1,0:T(8,128)(2,1)}, u32[]{:S(2)}, u32[]{:S(2)}) collective-permute-start(bf16[4,128,256]{2,1,0:T(8,128)(2,1)} %copy-done.18), channel_id=1, source_target_pairs={{0,1},{1,0},{2,3},{3,2},{4,5},{5,4},{6,7},{7,6},{8,9},{9,8},{10,11... | collective-permute-start | bytes 786440 | tf_op jit(solution)/shard_map/ppermute | solution.py:65
  155.4 47.1 %collective-permute-start.46 = (bf16[4,128,256]{2,1,0:T(8,128)(2,1)}, bf16[4,128,256]{2,1,0:T(8,128)(2,1)}, u32[]{:S(2)}, u32[]{:S(2)}) collective-permute-start(bf16[4,128,256]{2,1,0:T(8,128)(2,1)} %copy-done.21), channel_id=1, source_target_pairs={{0,1},{1,0},{2,3},{3,2},{4,5},{5,4},{6,7},{7,6},{8,9},{9,8},{10,11... | collective-permute-start | bytes 786440 | tf_op jit(solution)/shard_map/ppermute | solution.py:65
  (119 other events, 2356.8 us)
